TPU v7x, 256 devices: a whole 4x4x8 slice. The times are simulated.
256 devices in a mesh: seq: 32 (over x, y, core), mp: 8 (over z).
Axes of the slice: x: 4, y: 4, z: 8, core: 2. Of those that a mesh axis runs over, the one named last changes fastest.
Arguments:
- queries: bfloat16 [4096, 4096], P('seq', 'mp'), may hold values from -2 to 2
- keys: bfloat16 [4096, 4096], P('seq', 'mp'), may hold values from -2 to 2
- values: bfloat16 [4096, 4096], P('seq', 'mp'), may hold values from -6 to 6
- log_decay: float32 [32, 4096], P('mp', 'seq'), may hold values from -1.2 to 0
- residual: bfloat16 [4096, 6144], P(('seq', 'mp')), may hold values from -6 to 6
- out_weight: bfloat16 [4096, 6144], P('mp', 'seq'), may hold values from -0.09375 to 0.09375
- gate_weight: bfloat16 [32, 6144, 2304], P('seq', None, 'mp'), may hold values from -0.078125 to 0.078125
- up_weight: bfloat16 [32, 6144, 2304], P('seq', None, 'mp'), may hold values from -0.078125 to 0.078125
- down_weight: bfloat16 [32, 2304, 6144], P('seq', 'mp'), may hold values from -0.09375 to 0.09375
- expert_ids: int32 [4096, 2], P(('seq', 'mp')), may hold values from 0 to 15, all different within a row; in each aligned block of 16 rows (0 to 15, 16 to 31, ...) at most 3 rows name the same one
- route_weights: float32 [4096, 2], P(('seq', 'mp')), may hold values from 0.2 to 1
Outputs:
- output: bfloat16 [4096, 6144], P(('seq', 'mp'))
Inputs may be any that keep to these rules, and one draw needn't show every extreme that they name: `expert_ids`: the 2 experts of a token differ. Among the 16 tokens of one device (aligned blocks of rows in token order) no expert is named more than 3 times, a bound that some block reaches.
All inputs are finite; a program needn't handle non-finite values.
Results may differ from a plain program's by a relative error of at most 0.015.
Values may be sent and summed in bfloat16 or wider, within the bound.
A program may use at most 128 MiB of HBM per device.

v0:
```python
import jax
import jax.numpy as jnp
from jax import lax
from jax.sharding import PartitionSpec as P

TOP = 2
PAIR = 2


def per_device(
    queries,
    keys,
    values,
    log_decay,
    residual,
    out_weight,
    gate_weight,
    up_weight,
    down_weight,
    expert_ids,
    route_weights,
):
    seq_count = lax.axis_size("seq")
    span_len = queries.shape[0]
    head_count = log_decay.shape[0]
    head_size = queries.shape[1] // head_count
    query_heads = queries.reshape(span_len, head_count, head_size)
    key_heads = keys.reshape(span_len, head_count, head_size)
    value_heads = values.reshape(span_len, head_count, head_size)
    cumulative = jnp.cumsum(log_decay, axis=1)
    positions = jnp.arange(span_len)
    causal = (positions[:, None] >= positions[None, :])[None]
    spread_log = cumulative[:, :, None] - cumulative[:, None, :]
    weight = jnp.where(causal, jnp.exp(jnp.where(causal, spread_log, 0.0)), 0.0)
    raw_scores = jnp.einsum(
        "thd,shd->hts", query_heads, key_heads, preferred_element_type=jnp.float32
    )
    local_scores = (raw_scores * weight).astype(jnp.bfloat16)
    local_part = jnp.einsum(
        "hts,shd->thd", local_scores, value_heads, preferred_element_type=jnp.float32
    )
    span_total = cumulative[:, -1]
    key_scale = jnp.exp(span_total[:, None] - cumulative)
    weighted_keys = (key_scale.T[:, :, None] * key_heads.astype(jnp.float32)).astype(jnp.bfloat16)
    span_state = jnp.einsum(
        "thd,the->hde", weighted_keys, value_heads, preferred_element_type=jnp.float32
    ).astype(jnp.bfloat16)
    decays = lax.all_gather(span_total[None, :], "seq", axis=0, tiled=True)
    running = jnp.cumsum(decays, axis=0)
    my_index = lax.axis_index("seq")
    before = lax.dynamic_index_in_dim(running, jnp.maximum(my_index - 1, 0), 0, keepdims=False)
    shard_piece = lax.all_gather(span_state[None], "seq", axis=0, tiled=True)
    row_count = shard_piece.shape[0]
    source = jnp.arange(row_count)
    earlier_mask = (source < my_index)[:, None]
    factor = jnp.where(
        earlier_mask, jnp.exp(jnp.where(earlier_mask, before[None, :] - running, 0.0)), 0.0
    )
    prefix = jnp.einsum(
        "nh,nhde->hde", factor, shard_piece.astype(jnp.float32), precision=lax.Precision.HIGHEST
    )
    prefix_low = prefix.astype(jnp.bfloat16)
    weighted_queries = (jnp.exp(cumulative).T[:, :, None] * query_heads.astype(jnp.float32)).astype(
        jnp.bfloat16
    )
    carried_part = jnp.einsum(
        "thd,hde->the", weighted_queries, prefix_low, preferred_element_type=jnp.float32
    )
    mixed_heads = local_part + carried_part
    normed = (
        mixed_heads * lax.rsqrt(jnp.mean(mixed_heads * mixed_heads, axis=-1, keepdims=True) + 1e-06)
    ).astype(jnp.bfloat16)
    normed = normed.reshape(span_len, head_count * head_size)
    partial_out = jnp.dot(
        normed,
        lax.all_gather(out_weight, "seq", axis=1, tiled=True),
        preferred_element_type=jnp.float32,
    )
    attn_out = lax.psum_scatter(
        partial_out.astype(jnp.bfloat16), "mp", scatter_dimension=0, tiled=True
    ).astype(jnp.float32)
    hidden_state = (residual.astype(jnp.float32) + attn_out).astype(jnp.bfloat16)
    hidden_wide = hidden_state.astype(jnp.float32)
    moe_input = (
        hidden_wide * lax.rsqrt(jnp.mean(hidden_wide * hidden_wide, axis=-1, keepdims=True) + 1e-06)
    ).astype(jnp.bfloat16)
    model_width = residual.shape[1]
    experts = seq_count // PAIR
    tok_rows = residual.shape[0]
    capacity = max(2, tok_rows * TOP * 3 // (2 * experts))
    assign_count = tok_rows * TOP
    flat_ids = expert_ids.reshape(-1)
    expert_hot = (flat_ids[:, None] == jnp.arange(experts)[None, :]).astype(jnp.int32)
    slot_rank = jnp.sum((jnp.cumsum(expert_hot, axis=0) - expert_hot) * expert_hot, axis=1)
    target = flat_ids * capacity + slot_rank
    slot_hot = (target[:, None] == jnp.arange(experts * capacity)[None, :]).astype(jnp.float32)
    owner_hot = (
        (jnp.arange(assign_count) // TOP)[:, None] == jnp.arange(tok_rows)[None, :]
    ).astype(jnp.float32)
    dispatch_map = jnp.einsum("as,at->st", slot_hot, owner_hot).astype(jnp.bfloat16)
    packed = jnp.dot(dispatch_map, moe_input, preferred_element_type=jnp.float32).astype(
        jnp.bfloat16
    )
    outgoing = jnp.broadcast_to(
        packed.reshape(experts, 1, capacity, model_width), (experts, PAIR, capacity, model_width)
    )
    outgoing = outgoing.reshape(seq_count, capacity, model_width)
    incoming = lax.all_to_all(outgoing, "seq", split_axis=0, concat_axis=0, tiled=True)
    expert_rows = incoming.reshape(seq_count * capacity, model_width)
    gate_matrix = gate_weight[0]
    up_matrix = up_weight[0]
    down_matrix = down_weight[0]
    shard_piece = lax.all_gather(expert_rows, "mp", axis=0, tiled=True)
    gate_value = jnp.dot(shard_piece, gate_matrix, preferred_element_type=jnp.float32)
    lifted = jnp.dot(shard_piece, up_matrix, preferred_element_type=jnp.float32)
    hidden_rows = (jax.nn.silu(gate_value) * lifted).astype(jnp.bfloat16)
    half_out = lax.psum_scatter(
        jnp.dot(hidden_rows, down_matrix, preferred_element_type=jnp.float32).astype(jnp.bfloat16),
        "mp",
        scatter_dimension=0,
        tiled=True,
    )
    returned = lax.all_to_all(
        half_out.reshape(seq_count, capacity, model_width),
        "seq",
        split_axis=0,
        concat_axis=0,
        tiled=True,
    )
    expert_out = jnp.sum(
        returned.reshape(experts, PAIR, capacity, model_width).astype(jnp.float32), axis=1
    )
    expert_out = expert_out.reshape(experts * capacity, model_width)
    weighted = route_weights.reshape(-1)[:, None] * slot_hot
    combine_map = jnp.einsum("at,as->ts", owner_hot, weighted, precision=lax.Precision.HIGHEST)
    expert_mix = jnp.dot(combine_map, expert_out, precision=lax.Precision.HIGHEST)
    return (hidden_wide + expert_mix).astype(jnp.bfloat16)


def solution(mesh):
    placed = (
        P("seq", "mp"),
        P("seq", "mp"),
        P("seq", "mp"),
        P("mp", "seq"),
        P(("seq", "mp"), None),
        P("mp", "seq"),
        P("seq", None, "mp"),
        P("seq", None, "mp"),
        P("seq", "mp", None),
        P(("seq", "mp"), None),
        P(("seq", "mp"), None),
    )
    return jax.shard_map(
        per_device, mesh=mesh, in_specs=placed, out_specs=P(("seq", "mp"), None), check_vma=False
    )
```

profile of v0, /device:TPU:1, one launch (start us, length us, event | category | flops | bytes accessed | tf_op | source)
XLA Modules:
  0.0 486.5 jit_solution(14480048780253203327)
XLA Ops:
  6.5 0.0 copy-start
  6.5 0.0 all-gather.10.cloned.1.call-start
  6.5 1.1 reduce_window_sum.33
  7.7 0.0 copy-start.2
  7.7 0.2 slice_reduce_fusion
  7.9 0.6 exponential_bitcast_fusion.1
  8.5 1.7 copy.40
  10.1 1.8 convolution_convert_fusion.3
  11.9 0.0 all-gather.10.cloned.1.call-update
  11.9 0.0 all-gather.6.cloned.1.call-start
  12.0 0.7 all-gather.6.cloned.1.call-update
  12.7 0.0 reduce-scatter.3.cloned.1.call-start
  12.8 1.3 dynamic-slice
  14.6 0.2 dynamic-update-slice
  14.8 65.6 %all-reduce = f32[128]{0:T(128)S(1)} all-reduce(f32[128]{0:T(128)S(1)} %dynamic-update-slice), channel_id=2, replica_groups=mesh['seq'=32,'mp'=8] {'seq'}, use_global_device_ids=true, to_apply=%add | all-reduce | flops 128 | bytes 1024
  80.4 0.0 copy-done.2
  80.4 0.7 reshape.101
  81.1 0.8 reduce_window_sum.34
  81.9 0.0 copy-start.1
  81.9 0.6 copy-done.1
  82.5 0.6 iota_compare_fusion
  83.1 0.8 select_bitcast_fusion
  83.9 2.1 convolution_bitcast_fusion.1
  86.0 3.8 multiply_reduce_fusion
  89.8 1.7 copy.38
  91.5 1.4 multiply_reduce_fusion.1
  92.9 0.7 multiply_convert_fusion
  93.6 29.8 %all-gather.6.cloned.1.call-done = bf16[512,6144]{0,1:T(8,128)(2,1)} async-done(((bf16[512,192]{0,1:T(8,128)(2,1)}), bf16[512,6144]{0,1:T(8,128)(2,1)}) %all-gather.6.cloned.1.call-update) | async-done | bytes 6291472 | tf_op jit(solution)/shard_map/all_gather | solution.py:76
  123.4 6.2 %convolution_convert_fusion.1 = bf16[128,6144]{1,0:T(8,128)(2,1)} fusion(bf16[128,512]{0,1:T(8,128)(2,1)} %bitcast.79, bf16[512,6144]{0,1:T(8,128)(2,1)} %all-gather.6.cloned.1.call-done), kind=kOutput, calls=%fused_computation.2 | convolution fusion | flops 806092800 | bytes 7995392 | tf_op jit(solution)/shard_map/dot_general | solution.py:74
  129.6 0.0 reduce-scatter.3.cloned.1.call-update
  129.6 0.0 all-gather.8.cloned.1.call-start
  129.7 0.0 copy-done.4
  129.7 0.1 copy.30
  129.8 0.1 reshape.95
  129.9 0.0 copy-start.3
  129.9 0.6 copy-done.3
  130.5 0.7 fusion.49
  131.1 0.8 reduce_window_sum.35
  131.9 0.9 select_reduce_fusion
  132.8 0.7 and_select_fusion
  133.4 31.6 %reduce-scatter.3.cloned.1.call-done = bf16[16,6144]{1,0:T(8,128)(2,1)} async-done(((bf16[128,6144]{1,0:T(8,128)(2,1)}), bf16[16,6144]{1,0:T(8,128)(2,1)}) %reduce-scatter.3.cloned.1.call-update) | async-done | bytes 196624 | tf_op jit(solution)/shard_map/reduce_scatter | solution.py:79
  165.0 1.2 fusion.22
  166.2 2.4 convolution_convert_fusion.2
  168.7 2.1 broadcast_in_dim.65
  170.8 1.9 broadcast_in_dim.66
  172.6 34.2 %all_to_all.10 = bf16[32,3,6144]{2,1,0:T(4,128)(2,1)} all-to-all(bf16[32,3,6144]{2,1,0:T(4,128)(2,1)S(1)} %bitcast.77), channel_id=1, replica_groups=mesh['seq'=32,'mp'=8] {'seq'}, dimensions={0} | all-to-all | bytes 2359296 | tf_op jit(solution)/shard_map/all_to_all | solution.py:108
  206.8 3.9 reshape.97
  210.7 0.0 all-gather.8.cloned.1.call-update
  210.8 0.2 reduce-scatter.5.cloned.1.call-start
  211.0 98.4 %all-gather.8.cloned.1.call-done = bf16[768,6144]{1,0:T(8,128)(2,1)} async-done(((bf16[96,6144]{1,0:T(8,128)(2,1)}), bf16[768,6144]{1,0:T(8,128)(2,1)}) %all-gather.8.cloned.1.call-update) | async-done | bytes 9437200 | tf_op jit(solution)/shard_map/all_gather | solution.py:113
  309.4 8.6 %fusion.4 = f32[768,288]{0,1:T(8,128)} fusion(bf16[768,6144]{1,0:T(8,128)(2,1)} %all-gather.8.cloned.1.call-done, bf16[1,6144,288]{1,2,0:T(8,128)(2,1)} %param.17), kind=kOutput, calls=%fused_computation.9 | convolution fusion | flops 2717908992 | bytes 13860864 | tf_op jit(solution)/shard_map/dot_general | solution.py:114
  317.9 0.0 copy-done
  317.9 15.0 %convolution_convert_fusion = bf16[768,6144]{1,0:T(8,128)(2,1)} fusion(bf16[1,288,6144]{2,1,0:T(8,128)(2,1)S(1)} %copy-done, bf16[768,6144]{1,0:T(8,128)(2,1)} %all-gather.8.cloned.1.call-done, bf16[1,6144,288]{1,2,0:T(8,128)(2,1)} %param.18, f32[768,288]{0,1:T(8,128)} %fusion.4), kind=kOutput, calls=%fused_computation | convolution fusion | flops 5441863680 | bytes 26836992 | tf_op jit(solution)/shard_map/dot_general | solution.py:118
  333.0 0.0 reduce-scatter.5.cloned.1.call-update
  333.0 103.7 %reduce-scatter.5.cloned.1.call-done = bf16[96,6144]{1,0:T(8,128)(2,1)} async-done(((bf16[768,6144]{1,0:T(8,128)(2,1)}), bf16[96,6144]{1,0:T(8,128)(2,1)}) %reduce-scatter.5.cloned.1.call-update) | async-done | bytes 1179664 | tf_op jit(solution)/shard_map/reduce_scatter | solution.py:117
  436.7 3.8 reshape.98
  440.5 7.7 %all-to-all-start.1 = ((bf16[32,3,6144]{2,1,0:T(4,128)(2,1)}), bf16[32,3,6144]{2,1,0:T(4,128)(2,1)}, u32[]{:S(2)}, u32[]{:S(2)}) async-start(bf16[32,3,6144]{2,1,0:T(4,128)(2,1)} %reshape.98), calls=%async_computation.3 | async-start | bytes 3145728 | tf_op jit(solution)/shard_map/all_to_all | solution.py:123
  448.1 0.8 copy.31
  448.9 0.6 mul.82
  449.5 0.9 fusion.47
  450.4 20.4 %all-to-all-done.1 = bf16[32,3,6144]{2,1,0:T(4,128)(2,1)} async-done(((bf16[32,3,6144]{2,1,0:T(4,128)(2,1)}), bf16[32,3,6144]{2,1,0:T(4,128)(2,1)}, u32[]{:S(2)}, u32[]{:S(2)}) %all-to-all-start.1) | async-done | bytes 1179680 | tf_op jit(solution)/shard_map/all_to_all | solution.py:123
  470.9 3.9 convert_reduce_fusion
  474.7 2.5 reshape.99
  477.3 2.7 fusion
  (7 shorter events, 0.0 us)
Async XLA Ops:
  6.5 311.4 %copy-start = (bf16[1,288,6144]{2,1,0:T(8,128)(2,1)S(1)}, bf16[1,288,6144]{2,1,0:T(8,128)(2,1)}, u32[]{:S(2)}) copy-start(bf16[1,288,6144]{2,1,0:T(8,128)(2,1)} %param.19) | copy-start | bytes 10616836
  6.5 79.5 %all-gather.10.cloned.1.call-start = ((), (), s32[]{:S(2)}) async-start(), calls=%async_computation.8 | async-start | bytes 4325376 | tf_op jit(solution)/shard_map/all_gather | solution.py:52
  7.7 72.7 %copy-start.2 = (f32[4,128]{1,0:T(4,128)}, f32[4,128]{1,0:T(4,128)S(1)}, u32[]{:S(2)}) copy-start(f32[4,128]{1,0:T(4,128)S(1)} %reduce_window_sum.33) | copy-start | bytes 6148
  11.9 111.4 %all-gather.6.cloned.1.call-start = ((), (), s32[]{:S(2)}) async-start(), calls=%async_computation.4 | async-start | bytes 6488064 | tf_op jit(solution)/shard_map/all_gather | solution.py:76
  12.7 152.3 %reduce-scatter.3.cloned.1.call-start = ((), (), s32[]{:S(2)}) async-start(), calls=%async_computation.5 | async-start | bytes 1769472 | tf_op jit(solution)/shard_map/reduce_scatter | solution.py:79
  81.9 0.6 copy-start.1
  123.4 6.3 %copy-start.4 = (s32[16,2]{0,1:T(2,128)S(1)}, s32[16,2]{0,1:T(2,128)}, u32[]{:S(2)}) copy-start(s32[16,2]{0,1:T(2,128)} %param.20) | copy-start | bytes 388
  129.6 179.7 %all-gather.8.cloned.1.call-start = ((), (), s32[]{:S(2)}) async-start(), calls=%async_computation.6 | async-start | bytes 10616832 | tf_op jit(solution)/shard_map/all_gather | solution.py:113
  129.9 0.6 copy-start.3
  210.8 225.9 %reduce-scatter.5.cloned.1.call-start = ((), (), s32[]{:S(2)}) async-start(), calls=%async_computation.7 | async-start | bytes 10616832 | tf_op jit(solution)/shard_map/reduce_scatter | solution.py:117
  440.5 30.4 %all-to-all-start.1 = ((bf16[32,3,6144]{2,1,0:T(4,128)(2,1)}), bf16[32,3,6144]{2,1,0:T(4,128)(2,1)}, u32[]{:S(2)}, u32[]{:S(2)}) async-start(bf16[32,3,6144]{2,1,0:T(4,128)(2,1)} %reshape.98), calls=%async_computation.3 | async-start | bytes 3145728 | tf_op jit(solution)/shard_map/all_to_all | solution.py:123
Sparse Core Ops, SparseCore 0:
  12.1 55.2 all-gather.9
  69.9 53.4 all-gather.5
  129.7 35.2 reduce-scatter.2
  210.9 98.4 all-gather.7
  333.1 103.5 reduce-scatter.4
where the time goes:
time: 487 us
  waiting for transfers between devices  285 us (59%)
  blocking collectives  99.8 us (20%)
  matrix products  41.2 us (8%)
  local copies, waits for them, and re-layouts  22.6 us (5%)
  other arithmetic  16.5 us (3%)
  between operations  13.8 us (3%)
  starting transfers between devices  8.01 us (2%)
    reduce_scatter x1, waiting for transfers between devices, per_device(): lax.psum_scatter(jnp.dot(hidden_rows, down_matrix, preferred_element_type...  104 us
    all_gather x1, waiting for transfers between devices, per_device(): shard_piece = lax.all_gather(expert_rows, 'mp', axis=0, tiled=True)  98.4 us
    unnamed x1, blocking collectives  65.6 us
    all_to_all x1, blocking collectives, per_device(): lax.all_to_all(outgoing, 'seq', split_axis=0, concat_axis=0, tiled=True)  34.2 us
    reduce_scatter x1, waiting for transfers between devices, per_device(): lax.psum_scatter(partial_out.astype(jnp.bfloat16), 'mp', scatter_dimensio...  31.6 us
    all_gather x1, waiting for transfers between devices, per_device(): lax.all_gather(out_weight, 'seq', axis=1, tiled=True)  29.8 us
    all_to_all x1, waiting for transfers between devices, per_device(): lax.all_to_all(half_out.reshape(seq_count, capacity, model_width), 'seq',...  20.4 us
    dot_general x1, matrix products, per_device(): jnp.dot(hidden_rows, down_matrix, preferred_element_type=jnp.float32)  15 us
  transfers between devices with their start and end apart: 6, of which 5 were waited for; matrix products, arithmetic and copies ran while one was open for 4% of the time, Pallas kernels for 0%

commit v1 on v0

--- a/solution.py
+++ b/solution.py
@@ -73,7 +73,9 @@
     normed = normed.reshape(span_len, head_count * head_size)
     partial_out = jnp.dot(
         normed,
-        lax.all_gather(out_weight, "seq", axis=1, tiled=True),
+        jnp.concatenate(
+            lax.all_to_all(jnp.stack([out_weight] * lax.axis_size("seq")), "seq", 0, 0), axis=1
+        ),
         preferred_element_type=jnp.float32,
     )
     attn_out = lax.psum_scatter(

time: 487 us -> 538 us (1.10)
  blocking collectives: 99.8 us -> 165 us
  waiting for transfers between devices: 285 us -> 257 us
  starting transfers between devices: 8.01 us -> 16.7 us
    unnamed x1, blocking collectives: 65.6 us -> 131 us
    all_gather x1 -> x0, waiting for transfers between devices: 29.8 us -> none  [per_device(): lax.all_gather(out_weight, 'seq', axis=1, tiled=True)]
    all_to_all x0 -> x1, starting transfers between devices: none -> 8.76 us  [per_device(): lax.all_to_all(jnp.stack([out_weight] * lax.axis_size('seq')), 'seq', 0, 0)]
  transfers between devices with their start and end apart: 6 -> 6, of which waited for: 5 -> 4; matrix products, arithmetic and copies ran while one was open for 4% -> 4% of each run, Pallas kernels for 0% -> 0%
where the time goes in v1:
time: 538 us; the launch traced here: 537 us
  waiting for transfers between devices  257 us (48%)
  blocking collectives  165 us (31%)
  matrix products  41.2 us (8%)
  local copies, waits for them, and re-layouts  26.3 us (5%)
  starting transfers between devices  16.7 us (3%)
  other arithmetic  16.4 us (3%)
  between operations  13.9 us (3%)
    unnamed x1, blocking collectives  131 us
    reduce_scatter x1, waiting for transfers between devices, per_device(): lax.psum_scatter(jnp.dot(hidden_rows, down_matrix, preferred_element_type...  104 us
    all_gather x1, waiting for transfers between devices, per_device(): shard_piece = lax.all_gather(expert_rows, 'mp', axis=0, tiled=True)  98.4 us
    reduce_scatter x1, waiting for transfers between devices, per_device(): lax.psum_scatter(partial_out.astype(jnp.bfloat16), 'mp', scatter_dimensio...  34.4 us
    all_to_all x1, blocking collectives, per_device(): lax.all_to_all(outgoing, 'seq', split_axis=0, concat_axis=0, tiled=True)  34.1 us
    all_to_all x1, waiting for transfers between devices, per_device(): lax.all_to_all(half_out.reshape(seq_count, capacity, model_width), 'seq',...  20.4 us
    dot_general x1, matrix products, per_device(): jnp.dot(hidden_rows, down_matrix, preferred_element_type=jnp.float32)  15 us
  transfers between devices with their start and end apart: 6, of which 4 were waited for; matrix products, arithmetic and copies ran while one was open for 4% of the time, Pallas kernels for 0%

profile of v1, /device:TPU:1, one launch (start us, length us, event | category | flops | bytes accessed | tf_op | source)
XLA Modules:
  0.0 536.8 jit_solution(394662826945822308)
XLA Ops:
  6.5 0.0 copy-start
  6.5 0.0 all-gather.7.cloned.1.call-start
  6.5 1.1 reduce_window_sum.33
  7.7 0.0 copy-start.2
  7.7 0.2 slice_reduce_fusion
  7.9 0.6 exponential_bitcast_fusion.1
  8.4 1.7 copy.41
  10.1 1.8 convolution_convert_fusion.3
  11.9 0.0 all-gather.7.cloned.1.call-update
  11.9 4.3 stack.2
  16.2 0.0 copy-done.2
  16.2 8.8 %all-to-all-start = ((bf16[32,512,192]{1,2,0:T(8,128)(2,1)}), bf16[32,512,192]{1,2,0:T(8,128)(2,1)}, u32[]{:S(2)}, u32[]{:S(2)}) async-start(bf16[32,512,192]{1,2,0:T(8,128)(2,1)} %stack.2), calls=%async_computation | async-start | bytes 12582912 | tf_op jit(solution)/shard_map/all_to_all | solution.py:77
  25.0 0.0 reduce-scatter.3.cloned.1.call-start
  25.1 0.0 copy-done.5
  25.1 0.6 dynamic-slice
  26.3 0.2 dynamic-update-slice
  26.6 131.2 %all-reduce = f32[128]{0:T(128)S(1)} all-reduce(f32[128]{0:T(128)S(1)} %dynamic-update-slice), channel_id=2, replica_groups=mesh['seq'=32,'mp'=8] {'seq'}, use_global_device_ids=true, to_apply=%add | all-reduce | flops 128 | bytes 1024
  157.8 0.7 reshape.111
  158.5 0.8 reduce_window_sum.34
  159.3 0.6 copy-done.1
  159.9 0.6 iota_compare_fusion
  160.5 0.8 select_bitcast_fusion
  161.3 2.1 convolution_bitcast_fusion.1
  163.4 3.7 multiply_reduce_fusion
  167.2 1.7 copy.39
  168.8 1.4 multiply_reduce_fusion.1
  170.2 0.7 multiply_convert_fusion
  170.9 0.0 all-to-all-done
  170.9 6.2 %convolution_convert_fusion.1 = bf16[128,6144]{1,0:T(8,128)(2,1)} fusion(bf16[128,512]{0,1:T(8,128)(2,1)} %bitcast.82, bf16[512,6144]{0,1:T(8,128)(2,1)} %bitcast.12), kind=kOutput, calls=%fused_computation.2 | convolution fusion | flops 806092800 | bytes 7995392 | tf_op jit(solution)/shard_map/dot_general | solution.py:74
  177.1 0.0 reduce-scatter.3.cloned.1.call-update
  177.1 0.0 all-gather.5.cloned.1.call-start
  177.2 0.0 copy-done.4
  177.2 0.1 copy.31
  177.3 0.1 reshape.105
  177.4 0.0 copy-start.3
  177.4 0.6 copy-done.3
  178.0 0.7 fusion.49
  178.7 0.8 reduce_window_sum.35
  179.4 0.9 select_reduce_fusion
  180.3 0.7 and_select_fusion
  181.0 34.4 %reduce-scatter.3.cloned.1.call-done = bf16[16,6144]{1,0:T(8,128)(2,1)} async-done(((bf16[128,6144]{1,0:T(8,128)(2,1)}), bf16[16,6144]{1,0:T(8,128)(2,1)}) %reduce-scatter.3.cloned.1.call-update) | async-done | bytes 196624 | tf_op jit(solution)/shard_map/reduce_scatter | solution.py:81
  215.3 1.2 fusion.22
  216.5 2.4 convolution_convert_fusion.2
  219.0 2.1 broadcast_in_dim.65
  221.1 1.9 broadcast_in_dim.66
  222.9 34.1 %all_to_all.15 = bf16[32,3,6144]{2,1,0:T(4,128)(2,1)} all-to-all(bf16[32,3,6144]{2,1,0:T(4,128)(2,1)S(1)} %bitcast.80), channel_id=1, replica_groups=mesh['seq'=32,'mp'=8] {'seq'}, dimensions={0} | all-to-all | bytes 2359296 | tf_op jit(solution)/shard_map/all_to_all | solution.py:110
  257.0 3.9 reshape.107
  261.0 0.0 all-gather.5.cloned.1.call-update
  261.0 0.2 reduce-scatter.5.cloned.1.call-start
  261.2 98.4 %all-gather.5.cloned.1.call-done = bf16[768,6144]{1,0:T(8,128)(2,1)} async-done(((bf16[96,6144]{1,0:T(8,128)(2,1)}), bf16[768,6144]{1,0:T(8,128)(2,1)}) %all-gather.5.cloned.1.call-update) | async-done | bytes 9437200 | tf_op jit(solution)/shard_map/all_gather | solution.py:115
  359.6 8.5 %fusion.4 = f32[768,288]{0,1:T(8,128)} fusion(bf16[768,6144]{1,0:T(8,128)(2,1)} %all-gather.5.cloned.1.call-done, bf16[1,6144,288]{1,2,0:T(8,128)(2,1)} %param.17), kind=kOutput, calls=%fused_computation.9 | convolution fusion | flops 2717908992 | bytes 13860864 | tf_op jit(solution)/shard_map/dot_general | solution.py:116
  368.2 0.0 copy-done
  368.2 15.0 %convolution_convert_fusion = bf16[768,6144]{1,0:T(8,128)(2,1)} fusion(bf16[1,288,6144]{2,1,0:T(8,128)(2,1)S(1)} %copy-done, bf16[768,6144]{1,0:T(8,128)(2,1)} %all-gather.5.cloned.1.call-done, bf16[1,6144,288]{1,2,0:T(8,128)(2,1)} %param.18, f32[768,288]{0,1:T(8,128)} %fusion.4), kind=kOutput, calls=%fused_computation | convolution fusion | flops 5441863680 | bytes 26836992 | tf_op jit(solution)/shard_map/dot_general | solution.py:120
  383.2 0.0 reduce-scatter.5.cloned.1.call-update
  383.3 103.7 %reduce-scatter.5.cloned.1.call-done = bf16[96,6144]{1,0:T(8,128)(2,1)} async-done(((bf16[768,6144]{1,0:T(8,128)(2,1)}), bf16[96,6144]{1,0:T(8,128)(2,1)}) %reduce-scatter.5.cloned.1.call-update) | async-done | bytes 1179664 | tf_op jit(solution)/shard_map/reduce_scatter | solution.py:119
  487.0 3.8 reshape.108
  490.8 7.6 %all-to-all-start.2 = ((bf16[32,3,6144]{2,1,0:T(4,128)(2,1)}), bf16[32,3,6144]{2,1,0:T(4,128)(2,1)}, u32[]{:S(2)}, u32[]{:S(2)}) async-start(bf16[32,3,6144]{2,1,0:T(4,128)(2,1)} %reshape.108), calls=%async_computation.4 | async-start | bytes 3145728 | tf_op jit(solution)/shard_map/all_to_all | solution.py:125
  498.4 0.8 copy.32
  499.2 0.6 mul.82
  499.8 0.9 fusion.47
  500.7 20.4 %all-to-all-done.2 = bf16[32,3,6144]{2,1,0:T(4,128)(2,1)} async-done(((bf16[32,3,6144]{2,1,0:T(4,128)(2,1)}), bf16[32,3,6144]{2,1,0:T(4,128)(2,1)}, u32[]{:S(2)}, u32[]{:S(2)}) %all-to-all-start.2) | async-done | bytes 1179680 | tf_op jit(solution)/shard_map/all_to_all | solution.py:125
  521.1 3.9 convert_reduce_fusion
  525.0 2.5 reshape.109
  527.5 2.7 fusion
  (9 shorter events, 0.0 us)
Async XLA Ops:
  6.5 361.7 %copy-start = (bf16[1,288,6144]{2,1,0:T(8,128)(2,1)S(1)}, bf16[1,288,6144]{2,1,0:T(8,128)(2,1)}, u32[]{:S(2)}) copy-start(bf16[1,288,6144]{2,1,0:T(8,128)(2,1)} %param.19) | copy-start | bytes 10616836
  6.5 156.9 %all-gather.7.cloned.1.call-start = ((), (), s32[]{:S(2)}) async-start(), calls=%async_computation.8 | async-start | bytes 4325376 | tf_op jit(solution)/shard_map/all_gather | solution.py:52
  7.7 8.6 %copy-start.2 = (f32[4,128]{1,0:T(4,128)}, f32[4,128]{1,0:T(4,128)S(1)}, u32[]{:S(2)}) copy-start(f32[4,128]{1,0:T(4,128)S(1)} %reduce_window_sum.33) | copy-start | bytes 6148
  16.2 8.8 %copy-start.5 = (u32[256]{0:T(256)S(1)}, u32[256]{0:T(256)}, u32[]{:S(2)}) copy-start(u32[256]{0:T(256)} %constant.66) | copy-start | bytes 3076
  16.2 154.7 %all-to-all-start = ((bf16[32,512,192]{1,2,0:T(8,128)(2,1)}), bf16[32,512,192]{1,2,0:T(8,128)(2,1)}, u32[]{:S(2)}, u32[]{:S(2)}) async-start(bf16[32,512,192]{1,2,0:T(8,128)(2,1)} %stack.2), calls=%async_computation | async-start | bytes 12582912 | tf_op jit(solution)/shard_map/all_to_all | solution.py:77
  25.0 190.3 %reduce-scatter.3.cloned.1.call-start = ((), (), s32[]{:S(2)}) async-start(), calls=%async_computation.5 | async-start | bytes 1769472 | tf_op jit(solution)/shard_map/reduce_scatter | solution.py:81
  159.3 0.6 copy-start.1
  170.9 6.3 %copy-start.4 = (s32[16,2]{0,1:T(2,128)S(1)}, s32[16,2]{0,1:T(2,128)}, u32[]{:S(2)}) copy-start(s32[16,2]{0,1:T(2,128)} %param.20) | copy-start | bytes 388
  177.1 182.5 %all-gather.5.cloned.1.call-start = ((), (), s32[]{:S(2)}) async-start(), calls=%async_computation.6 | async-start | bytes 10616832 | tf_op jit(solution)/shard_map/all_gather | solution.py:115
  177.4 0.6 copy-start.3
  261.0 226.0 %reduce-scatter.5.cloned.1.call-start = ((), (), s32[]{:S(2)}) async-start(), calls=%async_computation.7 | async-start | bytes 10616832 | tf_op jit(solution)/shard_map/reduce_scatter | solution.py:119
  490.8 30.4 %all-to-all-start.2 = ((bf16[32,3,6144]{2,1,0:T(4,128)(2,1)}), bf16[32,3,6144]{2,1,0:T(4,128)(2,1)}, u32[]{:S(2)}, u32[]{:S(2)}) async-start(bf16[32,3,6144]{2,1,0:T(4,128)(2,1)} %reshape.108), calls=%async_computation.4 | async-start | bytes 3145728 | tf_op jit(solution)/shard_map/all_to_all | solution.py:125
Sparse Core Ops, SparseCore 0:
  12.1 102.6 all-gather.6
  177.3 38.0 reduce-scatter.2
  261.1 98.4 all-gather.4
  383.4 103.5 reduce-scatter.4
